TPU v7x, 32 devices: a whole 2x2x4 slice. The times are simulated.
32 devices in a mesh: row: 8 (over z, y), col: 4 (over x, core).
Axes of the slice: x: 2, y: 2, z: 4, core: 2. Of those that a mesh axis runs over, the one named last changes fastest.
Arguments:
- env: float32 [512, 32768], P('row', 'col'), may hold values from -0.03125 to 0.03125
- wave: float32 [32768, 512], P('row', 'col'), may hold values from -6 to 6
- mpo: float32 [16, 16], replicated, may hold values from -1.5 to 1.5
Outputs:
- applied: float32 [512, 512], P('row', 'col')
All inputs are finite; a program needn't handle non-finite values.
Results may differ from a plain program's by a relative error of at most 0.00007.
Values sent between devices are 32-bit elements; how exact they have to be, the bound alone decides.
No kernel may reach another device: no remote copies, remote signals or barrier semaphores. Data moves between devices by JAX's collectives and lax.ppermute only.
A program may use at most 128 MiB of HBM per device.

v0:
```python
import jax
import jax.numpy as jnp
from jax import lax
from jax.sharding import PartitionSpec as P


def shards(env, wave, mpo):
    spins = mpo.shape[0]
    env_full = lax.all_gather(env, "col", axis=1, tiled=True)
    right_local = wave.shape[1] // spins
    partial_out = jnp.dot(
        env_full,
        lax.all_gather(wave, "row", axis=0, tiled=True),
        precision=lax.Precision.HIGHEST,
        preferred_element_type=jnp.float32,
    )
    out3 = partial_out.reshape(env.shape[0], right_local, spins)
    mixed = jnp.einsum("irs,st->itr", out3, mpo, precision=lax.Precision.HIGHEST)
    spun = lax.all_to_all(mixed, "col", split_axis=1, concat_axis=2, tiled=True)
    return spun.reshape(env.shape[0], -1)


def solution(mesh):
    in_specs = (P("row", "col"), P("row", "col"), P())
    out_specs = P("row", "col")
    return jax.shard_map(shards, mesh=mesh, in_specs=in_specs, out_specs=out_specs, check_vma=False)
```

profile of v0, /device:TPU:0, one launch (start us, length us, event | category | flops | bytes accessed | tf_op | source)
XLA Modules:
  0.0 345.3 jit_solution(17700859789182060455)
XLA Ops:
  6.5 0.0 copy-start
  6.5 0.0 all-gather.3.cloned.1.call-start
  6.5 0.7 all-gather.3.cloned.1.call-update
  7.3 0.0 all-gather.5.cloned.1.call-start
  7.3 0.7 all-gather.5.cloned.1.call-update
  8.0 61.9 %all-gather.3.cloned.1.call-done = f32[64,32768]{1,0:T(8,128)} async-done(((f32[64,8192]{1,0:T(8,128)}), f32[64,32768]{1,0:T(8,128)}) %all-gather.3.cloned.1.call-update) | async-done | bytes 8388624 | tf_op jit(solution)/shard_map/all_gather | solution.py:9
  69.9 229.4 %all-gather.5.cloned.1.call-done = f32[32768,128]{1,0:T(8,128)} async-done(((f32[4096,128]{1,0:T(8,128)}), f32[32768,128]{1,0:T(8,128)}) %all-gather.5.cloned.1.call-update) | async-done | bytes 16777232 | tf_op jit(solution)/shard_map/all_gather | solution.py:13
  299.4 30.2 %fusion.1 = f32[64,128]{0,1:T(8,128)S(1)} fusion(f32[64,32768]{1,0:T(8,128)} %all-gather.3.cloned.1.call-done, f32[32768,128]{1,0:T(8,128)} %all-gather.5.cloned.1.call-done), kind=kOutput, calls=%fused_computation.3 | convolution fusion | flops 3221225472 | bytes 25198592 | tf_op jit(solution)/shard_map/dot_general | solution.py:11
  329.5 0.0 copy-done
  329.5 0.3 convolution_bitcast_fusion
  329.8 0.1 reshape.10
  329.9 6.5 %all_to_all.15 = f32[4,1,2048]{2,1,0:T(1,128)S(1)} all-to-all(f32[4,1,2048]{2,1,0:T(1,128)S(1)} %reshape.10), channel_id=1, replica_groups=mesh['row'=8,'col'=4] {'col'}, dimensions={0} | all-to-all | bytes 65536 | tf_op jit(solution)/shard_map/all_to_all | solution.py:19
  336.4 0.5 broadcast
  336.9 0.7 reduce
  337.7 0.1 reshape.11
  337.8 0.7 copy.15
  (2 shorter events, 0.0 us)
Async XLA Ops:
  6.5 323.0 %copy-start = (f32[16,16]{1,0:T(8,128)S(1)}, f32[16,16]{1,0:T(8,128)}, u32[]{:S(2)}) copy-start(f32[16,16]{1,0:T(8,128)} %param.5) | copy-start | bytes 3076
  6.5 63.4 %all-gather.3.cloned.1.call-start = ((), (), s32[]{:S(2)}) async-start(), calls=%async_computation.1 | async-start | bytes 10485760 | tf_op jit(solution)/shard_map/all_gather | solution.py:9
  7.3 292.1 %all-gather.5.cloned.1.call-start = ((), (), s32[]{:S(2)}) async-start(), calls=%async_computation.2 | async-start | bytes 18874368 | tf_op jit(solution)/shard_map/all_gather | solution.py:13
Sparse Core Ops, SparseCore 0:
  8.9 60.9 all-gather.2
  72.0 227.2 all-gather.4
where the time goes:
time: 345 us
  waiting for transfers between devices  293 us (85%)
  matrix products  30.4 us (9%)
  between operations  13.4 us (4%)
  blocking collectives  6.49 us (2%)
    all_gather x1, waiting for transfers between devices, shards(): lax.all_gather(wave, 'row', axis=0, tiled=True)  229 us
    all_gather x1, waiting for transfers between devices, shards(): env_full = lax.all_gather(env, 'col', axis=1, tiled=True)  61.9 us
    dot_general x1, matrix products, shards(): jnp.dot(env_full, lax.all_gather(wave, 'row', axis=0, tiled=True), precis...  30.2 us
  transfers between devices with their start and end apart: 2, of which 2 were waited for; matrix products, arithmetic and copies ran while one was open for 0% of the time, Pallas kernels for 0%

commit v1 on v0

--- a/solution.py
+++ b/solution.py
@@ -6,7 +6,12 @@
 
 def shards(env, wave, mpo):
     spins = mpo.shape[0]
-    env_full = lax.all_gather(env, "col", axis=1, tiled=True)
+    ring = [env]
+    for hop in range(3):
+        ring.append(lax.ppermute(ring[-1], "col", [(dev, (dev + 1) % 4) for dev in range(4)]))
+    env_full = jnp.roll(
+        jnp.concatenate(ring[::-1], axis=1), (lax.axis_index("col") + 1) * ring[0].shape[1], axis=1
+    )
     right_local = wave.shape[1] // spins
     partial_out = jnp.dot(
         env_full,

time: 345 us -> 286 us (0.83)
  waiting for transfers between devices: 293 us -> 209 us
  local copies, waits for them, and re-layouts: 1.44 us -> 24.6 us
    all_gather x1, waiting for transfers between devices: 229 us -> 131 us  [shards(): lax.all_gather(wave, 'row', axis=0, tiled=True)]
    ppermute x0 -> x3, waiting for transfers between devices: none -> 77.1 us  [shards(): lax.ppermute(ring[-1], 'col', [(dev, (dev + 1) % 4) for dev in range(4)])]
    all_gather x1 -> x0, waiting for transfers between devices: 61.9 us -> none  [shards(): env_full = lax.all_gather(env, 'col', axis=1, tiled=True)]
    unnamed x4 -> x17, local copies, waits for them, and re-layouts: 0.2 us -> 22 us
  transfers between devices with their start and end apart: 2 -> 4, of which waited for: 2 -> 4; matrix products, arithmetic and copies ran while one was open for 0% -> 8% of each run, Pallas kernels for 0% -> 0%
where the time goes in v1:
time: 286 us; the launch traced here: 285 us
  waiting for transfers between devices  209 us (73%)
  matrix products  30.4 us (11%)
  local copies, waits for them, and re-layouts  24.6 us (9%)
  between operations  13.4 us (5%)
  blocking collectives  6.48 us (2%)
    all_gather x1, waiting for transfers between devices, shards(): lax.all_gather(wave, 'row', axis=0, tiled=True)  131 us
    ppermute x3, waiting for transfers between devices, shards(): lax.ppermute(ring[-1], 'col', [(dev, (dev + 1) % 4) for dev in range(4)])  77.1 us
    dot_general x1, matrix products, shards(): jnp.dot(env_full, lax.all_gather(wave, 'row', axis=0, tiled=True), precis...  30.2 us
    unnamed x17, local copies, waits for them, and re-layouts  22 us
    all_to_all x1, blocking collectives, shards(): spun = lax.all_to_all(mixed, 'col', split_axis=1, concat_axis=2, tiled=True)  6.48 us
  transfers between devices with their start and end apart: 4, of which 4 were waited for; matrix products, arithmetic and copies ran while one was open for 8% of the time, Pallas kernels for 0%

profile of v1, /device:TPU:0, one launch (start us, length us, event | category | flops | bytes accessed | tf_op | source)
XLA Modules:
  0.0 285.5 jit_solution(1375108238469908680)
XLA Ops:
  6.5 0.0 copy-start
  6.5 0.0 copy-start.1
  6.5 0.0 all-gather.2.cloned.1.call-start
  6.5 0.7 all-gather.2.cloned.1.call-update
  7.3 0.5 collective-permute-start
  7.8 25.8 %collective-permute-done = f32[64,8192]{1,0:T(8,128)S(1)} collective-permute-done((f32[64,8192]{1,0:T(8,128)}, f32[64,8192]{1,0:T(8,128)S(1)}, u32[]{:S(2)}, u32[]{:S(2)}) %collective-permute-start) | collective-permute-done | bytes 2097184 | tf_op jit(solution)/shard_map/ppermute | solution.py:11
  33.7 0.0 copy-start.2
  33.7 1.3 copy-done.2
  35.0 0.0 collective-permute-start.1
  35.0 25.5 %collective-permute-done.1 = f32[64,8192]{1,0:T(8,128)} collective-permute-done((f32[64,8192]{1,0:T(8,128)S(1)}, f32[64,8192]{1,0:T(8,128)}, u32[]{:S(2)}, u32[]{:S(2)}) %collective-permute-start.1) | collective-permute-done | bytes 2097184 | tf_op jit(solution)/shard_map/ppermute | solution.py:11
  60.6 0.0 collective-permute-start.2
  60.6 0.0 copy-start.3
  60.6 25.8 %collective-permute-done.2 = f32[64,8192]{1,0:T(8,128)} collective-permute-done((f32[64,8192]{1,0:T(8,128)}, f32[64,8192]{1,0:T(8,128)}, u32[]{:S(2)}, u32[]{:S(2)}) %collective-permute-start.2) | collective-permute-done | bytes 2097184 | tf_op jit(solution)/shard_map/ppermute | solution.py:11
  86.3 3.0 %constant_dynamic-update-slice_fusion.7 = f32[64,65536]{1,0:T(8,128)} fusion(f32[64,8192]{1,0:T(8,128)} %collective-permute-done.2), kind=kLoop, calls=%fused_computation.10 | loop fusion | bytes 4194304
  89.4 3.0 %constant_dynamic-update-slice_fusion.6 = f32[64,65536]{1,0:T(8,128)} fusion(f32[64,65536]{1,0:T(8,128)} %constant_dynamic-update-slice_fusion.7, f32[64,8192]{1,0:T(8,128)} %collective-permute-done.1), kind=kLoop, calls=%fused_computation.9 | loop fusion | bytes 4194304
  92.4 3.0 %constant_dynamic-update-slice_fusion.5 = f32[64,65536]{1,0:T(8,128)} fusion(f32[64,65536]{1,0:T(8,128)} %constant_dynamic-update-slice_fusion.6, f32[64,8192]{1,0:T(8,128)} %copy-done.2), kind=kLoop, calls=%fused_computation.8 | loop fusion | bytes 4194304
  95.4 3.1 %constant_dynamic-update-slice_fusion.4 = f32[64,65536]{1,0:T(8,128)} fusion(f32[64,65536]{1,0:T(8,128)} %constant_dynamic-update-slice_fusion.5, f32[64,8192]{1,0:T(8,128)} %param.3), kind=kLoop, calls=%fused_computation.7 | loop fusion | bytes 4194304
  98.5 3.6 %constant_dynamic-update-slice_fusion.3 = f32[64,65536]{1,0:T(8,128)} fusion(f32[64,65536]{1,0:T(8,128)} %constant_dynamic-update-slice_fusion.4, f32[64,8192]{1,0:T(8,128)} %collective-permute-done.2), kind=kLoop, calls=%fused_computation.6 | loop fusion | bytes 4194304
  102.1 3.2 %constant_dynamic-update-slice_fusion.2 = f32[64,65536]{1,0:T(8,128)} fusion(f32[64,65536]{1,0:T(8,128)} %constant_dynamic-update-slice_fusion.3, f32[64,8192]{1,0:T(8,128)} %collective-permute-done.1), kind=kLoop, calls=%fused_computation.5 | loop fusion | bytes 4194304
  105.4 0.0 copy-done.3
  105.4 1.4 constant_dynamic-update-slice_fusion.1
  106.8 0.0 copy-done.1
  106.8 1.4 constant_dynamic-update-slice_fusion
  108.2 131.3 %all-gather.2.cloned.1.call-done = f32[32768,128]{1,0:T(8,128)} async-done(((f32[4096,128]{1,0:T(8,128)}), f32[32768,128]{1,0:T(8,128)}) %all-gather.2.cloned.1.call-update) | async-done | bytes 16777232 | tf_op jit(solution)/shard_map/all_gather | solution.py:18
  239.5 30.2 %fusion = f32[64,128]{0,1:T(8,128)S(1)} fusion(f32[32768,128]{1,0:T(8,128)} %all-gather.2.cloned.1.call-done, f32[64,65536]{1,0:T(8,128)} %constant_dynamic-update-slice_fusion, s32[]{:T(128)S(6)} %select_n.14), kind=kOutput, calls=%fused_computation | convolution fusion | flops 3221225472 | bytes 25198596 | tf_op jit(solution)/shard_map/dot_general | solution.py:16
  269.7 0.0 copy-done
  269.7 0.3 convolution_bitcast_fusion
  270.0 0.1 reshape.10
  270.1 6.5 %all_to_all.15 = f32[4,1,2048]{2,1,0:T(1,128)S(1)} all-to-all(f32[4,1,2048]{2,1,0:T(1,128)S(1)} %reshape.10), channel_id=1, replica_groups=mesh['row'=8,'col'=4] {'col'}, dimensions={0} | all-to-all | bytes 65536 | tf_op jit(solution)/shard_map/all_to_all | solution.py:24
  276.6 0.5 broadcast.1
  277.1 0.7 reduce
  277.8 0.1 reshape.11
  277.9 0.7 copy.15
  (2 shorter events, 0.0 us)
Async XLA Ops:
  6.5 263.1 %copy-start = (f32[16,16]{1,0:T(8,128)S(1)}, f32[16,16]{1,0:T(8,128)}, u32[]{:S(2)}) copy-start(f32[16,16]{1,0:T(8,128)} %param.5) | copy-start | bytes 3076
  6.5 100.2 %copy-start.1 = (f32[64,8192]{1,0:T(8,128)S(1)}, f32[64,8192]{1,0:T(8,128)}, u32[]{:S(2)}) copy-start(f32[64,8192]{1,0:T(8,128)} %param.3) | copy-start | bytes 6291460
  6.5 233.0 %all-gather.2.cloned.1.call-start = ((), (), s32[]{:S(2)}) async-start(), calls=%async_computation.1 | async-start | bytes 18874368 | tf_op jit(solution)/shard_map/all_gather | solution.py:18
  7.3 26.4 %collective-permute-start = (f32[64,8192]{1,0:T(8,128)}, f32[64,8192]{1,0:T(8,128)S(1)}, u32[]{:S(2)}, u32[]{:S(2)}) collective-permute-start(f32[64,8192]{1,0:T(8,128)} %param.3), channel_id=1, source_target_pairs={{0,1},{1,2},{2,3},{3,0},{4,5},{5,6},{6,7},{7,4},{8,9},{9,10},{10,1... | collective-permute-start | bytes 6291464 | tf_op jit(solution)/shard_map/ppermute | solution.py:11
  33.7 1.3 copy-start.2
  35.0 25.6 %collective-permute-start.1 = (f32[64,8192]{1,0:T(8,128)S(1)}, f32[64,8192]{1,0:T(8,128)}, u32[]{:S(2)}, u32[]{:S(2)}) collective-permute-start(f32[64,8192]{1,0:T(8,128)S(1)} %collective-permute-done), channel_id=1, source_target_pairs={{0,1},{1,2},{2,3},{3,0},{4,5},{5,6},{6,7},{7,4},{8,9},{9,10},{10,1... | collective-permute-start | bytes 6291464 | tf_op jit(solution)/shard_map/ppermute | solution.py:11
  60.6 25.8 %collective-permute-start.2 = (f32[64,8192]{1,0:T(8,128)}, f32[64,8192]{1,0:T(8,128)}, u32[]{:S(2)}, u32[]{:S(2)}) collective-permute-start(f32[64,8192]{1,0:T(8,128)} %collective-permute-done.1), channel_id=1, source_target_pairs={{0,1},{1,2},{2,3},{3,0},{4,5},{5,6},{6,7},{7,4},{8,9},{9,10},{10,1... | collective-permute-start | bytes 6291464 | tf_op jit(solution)/shard_map/ppermute | solution.py:11
  60.6 44.8 %copy-start.3 = (f32[64,8192]{1,0:T(8,128)S(1)}, f32[64,8192]{1,0:T(8,128)}, u32[]{:S(2)}) copy-start(f32[64,8192]{1,0:T(8,128)} %copy-done.2) | copy-start | bytes 6291460
Sparse Core Ops, SparseCore 0:
  9.5 229.9 all-gather.1
